TPU v7x, 256 devices: a whole 4x4x8 slice. The times are simulated.
256 devices in a mesh: grp: 8 (over y, core), dev: 32 (over z, x).
Axes of the slice: x: 4, y: 4, z: 8, core: 2. Of those that a mesh axis runs over, the one named last changes fastest.
Arguments:
- video_in: bfloat16 [4, 256, 256, 1024], P(None, ('grp', 'dev')), may hold values from -24 to 24
- space_gain: float32 [1024], replicated, may hold values from 0.25 to 1.75
- space_project: bfloat16 [1024, 1536], replicated, may hold values from -6 to 6
- space_output: bfloat16 [512, 1024], replicated, may hold values from -0.25 to 0.25
- time_gain: float32 [1024], replicated, may hold values from 0.25 to 1.75
- time_project: bfloat16 [1024, 1536], replicated, may hold values from -6 to 6
- time_output: bfloat16 [512, 1024], replicated, may hold values from -0.25 to 0.25
Outputs:
- video_out: bfloat16 [4, 256, 256, 1024], P(None, ('grp', 'dev'))
All inputs are finite; a program needn't handle non-finite values.
Results may differ from a plain program's by a relative error of at most 0.007.
Values may be sent and summed in bfloat16 or wider, within the bound.
A program may use at most 128 MiB of HBM per device.

v0:
```python
import jax
import jax.numpy as jnp
from jax import lax
from jax.sharding import PartitionSpec as P

HEADS = 8
HEAD_DIM = 64


norm_epsilon = 1e-06
masked_score = -1e30


def layer_norm(activations, gain_vec):
    floats = activations.astype(jnp.float32)
    centre = jnp.mean(floats, axis=-1, keepdims=True)
    spread = jnp.mean(jnp.square(floats - centre), axis=-1, keepdims=True)
    return ((floats - centre) * lax.rsqrt(spread + norm_epsilon) * gain_vec).astype(jnp.bfloat16)


def soft_weights(scores, allowed):
    scores = jnp.where(allowed, scores, masked_score)
    top_score = jnp.max(scores, axis=-1, keepdims=True)
    exponent = jnp.where(allowed, jnp.exp(scores - top_score), 0.0)
    row_total = jnp.sum(exponent, axis=-1, keepdims=True)
    return (exponent / row_total).astype(jnp.bfloat16)


def spatial_layer(frame_view, space_gain, space_project, space_output):
    clip_count, patch_count, model_width = frame_view.shape
    attn_width = HEADS * HEAD_DIM
    normed = layer_norm(frame_view, space_gain)
    projected = jnp.dot(
        normed.reshape(-1, model_width), space_project, preferred_element_type=jnp.float32
    )
    projected = projected.astype(jnp.bfloat16).reshape(clip_count, patch_count, 3, HEADS, HEAD_DIM)
    queries = projected[:, :, 0]
    keys_all = projected[:, :, 1]
    values_all = projected[:, :, 2]
    score_scale = HEAD_DIM ** (-0.5)
    scores = (
        jnp.einsum("cqhe,ckhe->chqk", queries, keys_all, preferred_element_type=jnp.float32)
        * score_scale
    )
    allowed = jnp.ones((patch_count, patch_count), jnp.bool_)
    weights = soft_weights(scores, allowed)
    context = jnp.einsum(
        "chqk,ckhe->cqhe", weights, values_all, preferred_element_type=jnp.float32
    ).astype(jnp.bfloat16)
    update = jnp.dot(
        context.reshape(-1, attn_width), space_output, preferred_element_type=jnp.float32
    )
    return (
        frame_view.astype(jnp.float32) + update.reshape(clip_count, patch_count, model_width)
    ).astype(jnp.bfloat16)


def to_frames(sending, group_count, member_count, patch_count):
    clip_count = sending.shape[0]
    lane_width = sending.shape[-1]
    patch_here = sending.shape[2]
    sectioned = sending.reshape(clip_count, group_count, member_count, 1, 1, patch_here, lane_width)
    arrived = lax.all_to_all(
        lax.all_to_all(sectioned, "grp", split_axis=1, concat_axis=3, tiled=True),
        "dev",
        split_axis=2,
        concat_axis=4,
        tiled=True,
    )
    return arrived.reshape(clip_count, patch_count, lane_width)


def per_device(
    video_in, space_gain, space_project, space_output, time_gain, time_project, time_output
):
    clip_count, frame_local, patch_count, model_width = video_in.shape
    attn_width = HEADS * HEAD_DIM
    group_count = lax.axis_size("grp")
    member_count = lax.axis_size("dev")
    frame_view = video_in.reshape(clip_count, patch_count, model_width)
    mixed_rows = spatial_layer(frame_view, space_gain, space_project, space_output)
    sectioned = mixed_rows.reshape(clip_count, 1, 1, patch_count, model_width)
    arrived = lax.all_to_all(
        lax.all_to_all(sectioned, "grp", split_axis=3, concat_axis=1, tiled=True),
        "dev",
        split_axis=3,
        concat_axis=2,
        tiled=True,
    )
    local_rows = arrived.reshape(
        clip_count,
        group_count * member_count,
        patch_count // (group_count * member_count),
        model_width,
    )
    frame_here = local_rows.shape[1]
    patch_here = local_rows.shape[2]
    normed = layer_norm(local_rows, time_gain)
    projected = jnp.dot(
        normed.reshape(-1, model_width), time_project, preferred_element_type=jnp.float32
    )
    projected = projected.astype(jnp.bfloat16).reshape(
        clip_count, frame_here, patch_here, 3, HEADS, HEAD_DIM
    )
    queries = projected[:, :, :, 0]
    keys_here = projected[:, :, :, 1]
    values_here = projected[:, :, :, 2]
    query_frames = jnp.arange(frame_here)
    key_frames = jnp.arange(keys_here.shape[1])
    allowed = key_frames[None, :] <= query_frames[:, None]
    score_scale = HEAD_DIM ** (-0.5)
    scores = (
        jnp.einsum("cqphe,ckphe->cphqk", queries, keys_here, preferred_element_type=jnp.float32)
        * score_scale
    )
    weights = soft_weights(scores, allowed)
    context = jnp.einsum(
        "cphqk,ckphe->cqphe", weights, values_here, preferred_element_type=jnp.float32
    )
    context = context.astype(jnp.bfloat16).reshape(clip_count, frame_here, patch_here, attn_width)
    update = jnp.dot(
        context.reshape(-1, attn_width), time_output, preferred_element_type=jnp.float32
    )
    update_here = update.astype(jnp.bfloat16).reshape(
        clip_count, frame_here, patch_here, model_width
    )
    update_rows = to_frames(update_here, group_count, member_count, patch_count)
    result = (mixed_rows.astype(jnp.float32) + update_rows.astype(jnp.float32)).astype(jnp.bfloat16)
    return result.reshape(clip_count, frame_local, patch_count, model_width)


def solution(mesh):
    in_specs = (P(None, ("grp", "dev"), None, None), P(), P(), P(), P(), P(), P())
    out_specs = P(None, ("grp", "dev"), None, None)
    return jax.shard_map(
        per_device, mesh=mesh, in_specs=in_specs, out_specs=out_specs, check_vma=False
    )
```

profile of v0, /device:TPU:1, one launch (start us, length us, event | category | flops | bytes accessed | tf_op | source)
XLA Modules:
  0.0 269.9 jit_solution(4308138091376367578)
XLA Ops:
  0.0 0.0 copy-start
  0.0 2.1 convert_reduce_fusion
  2.1 2.4 fusion.13
  4.5 0.0 copy-done.2
  4.5 0.0 copy-done.8
  4.6 0.7 fusion.11
  5.2 0.0 copy-done
  5.3 4.9 %convolution_convert_fusion.1 = bf16[1024,1536]{1,0:T(8,128)(2,1)} fusion(bf16[1024,1024]{1,0:T(8,128)(2,1)S(1)} %fusion.11, bf16[1024,1536]{1,0:T(8,128)(2,1)S(1)} %copy-done), kind=kOutput, calls=%fused_computation.34 | convolution fusion | flops 3222798336 | bytes 8388608 | tf_op jit(solution)/shard_map/dot_general | solution.py:33
  10.1 8.9 %reshape.178 = bf16[4,256,3,8,64]{4,3,2,1,0:T(8,128)(2,1)} reshape(bf16[1024,1536]{1,0:T(8,128)(2,1)} %convolution_convert_fusion.1) | data formatting | bytes 6291456 | tf_op jit(solution)/shard_map/reshape | solution.py:36
  19.0 5.3 %fusion.40 = (bf16[4,256,1,8,64]{4,3,2,1,0:T(8,128)(2,1)}, bf16[4,256,1,8,64]{4,3,2,1,0:T(8,128)(2,1)}, bf16[4,256,1,8,64]{4,3,2,1,0:T(8,128)(2,1)S(1)}) fusion(bf16[4,256,3,8,64]{4,3,2,1,0:T(8,128)(2,1)} %reshape.178), kind=kLoop, calls=%fused_computation.61 | loop fusion | bytes 6291456 | tf_op jit(solution)/shard_map/slice | solution.py:39
  24.3 3.0 %copy.79 = bf16[4,256,1,8,64]{1,4,3,0,2:T(8,128)(2,1)} copy(bf16[4,256,1,8,64]{4,3,2,1,0:T(8,128)(2,1)} %get-tuple-element.8) | data formatting | bytes 2097152
  27.3 2.2 copy.80
  29.6 1.9 copy.81
  31.5 2.5 fusion.31
  34.0 0.0 copy-start.7
  34.0 6.3 %fusion.41 = (f32[4,8,256]{2,1,0:T(8,128)S(1)}, f32[4,8,256,256]{2,3,1,0:T(8,128)S(1)}) fusion(f32[4,8,256,256]{2,3,1,0:T(8,128)S(1)} %fusion.31), kind=kOutput, calls=%fused_computation.62 | output fusion | flops 8388863 | bytes 16809984 | tf_op jit(solution)/shard_map/sub | solution.py:24
  40.3 0.0 copy-done.7
  40.4 0.0 copy-start.3
  40.4 0.0 copy-start.11
  40.4 0.9 fusion.24
  41.3 0.6 copy-done.3
  41.9 0.3 copy-done.11
  42.2 1.3 fusion.14
  43.5 0.0 copy-start.4
  43.5 1.6 copy.59
  45.1 32.2 %all_to_all.48 = bf16[4,1,1,256,1024]{4,0,2,1,3:T(4,128)(2,1)S(1)} all-to-all(bf16[4,1,1,256,1024]{4,0,2,1,3:T(4,128)(2,1)S(1)} %copy.59), channel_id=1, replica_groups=mesh['grp'=8,'dev'=32] {'grp'}, dimensions={3} | all-to-all | bytes 4194304 | tf_op jit(solution)/shard_map/all_to_all | solution.py:84
  77.4 0.0 copy-done.4
  77.4 3.0 %copy.60 = bf16[4,8,1,32,1024]{4,1,0,2,3:T(8,128)(2,1)} copy(bf16[4,8,1,32,1024]{4,0,3,1,2:T(4,128)(2,1)S(1)} %bitcast.95) | data formatting | bytes 4194304 | tf_op jit(solution)/shard_map/all_to_all | solution.py:84
  80.4 11.2 %all-to-all-start.1 = ((bf16[4,8,1,32,1024]{4,1,0,2,3:T(8,128)(2,1)}), bf16[4,8,1,32,1024]{4,1,0,2,3:T(8,128)(2,1)S(1)}, u32[]{:S(2)}, u32[]{:S(2)}) async-start(bf16[4,8,1,32,1024]{4,1,0,2,3:T(8,128)(2,1)} %copy.60), calls=%async_computation.1 | async-start | bytes 4194304 | tf_op jit(solution)/shard_map/all_to_all | solution.py:83
  91.7 48.1 %all-to-all-done.1 = bf16[4,8,1,32,1024]{4,1,0,2,3:T(8,128)(2,1)S(1)} async-done(((bf16[4,8,1,32,1024]{4,1,0,2,3:T(8,128)(2,1)}), bf16[4,8,1,32,1024]{4,1,0,2,3:T(8,128)(2,1)S(1)}, u32[]{:S(2)}, u32[]{:S(2)}) %all-to-all-start.1) | async-done | bytes 2097184 | tf_op jit(solution)/shard_map/all_to_all | solution.py:83
  139.8 1.9 fusion.22
  141.7 0.1 div.39
  141.8 2.0 multiply_reduce_fusion.1
  143.8 0.1 rsqrt.25
  143.9 1.2 copy_convert_fusion
  145.1 0.0 copy-done.9
  145.1 0.0 copy-start.10
  145.2 0.6 fusion.8
  145.7 1.3 copy-done.10
  147.0 3.6 %convolution_convert_fusion = bf16[1024,1536]{1,0:T(8,128)(2,1)S(1)} fusion(bf16[1024,1024]{1,0:T(8,128)(2,1)S(1)} %fusion.8, bf16[1024,1536]{1,0:T(8,128)(2,1)S(1)} %copy-done.10), kind=kOutput, calls=%fused_computation.33 | convolution fusion | flops 3222798336 | bytes 8388608 | tf_op jit(solution)/shard_map/dot_general | solution.py:99
  150.7 5.9 %reshape.179 = bf16[4,256,1,3,8,64]{5,4,3,1,0,2:T(8,128)(2,1)} reshape(bf16[1024,1536]{1,0:T(8,128)(2,1)S(1)} %convolution_convert_fusion) | data formatting | bytes 6291456 | tf_op jit(solution)/shard_map/reshape | solution.py:102
  156.6 5.3 %fusion.39 = (bf16[4,256,1,1,8,64]{5,4,3,1,0,2:T(8,128)(2,1)}, bf16[4,256,1,1,8,64]{5,4,3,1,0,2:T(8,128)(2,1)}, bf16[4,256,1,1,8,64]{5,4,3,1,0,2:T(8,128)(2,1)S(1)}) fusion(bf16[4,256,1,3,8,64]{5,4,3,1,0,2:T(8,128)(2,1)} %reshape.179), kind=kLoop, calls=%fused_computation.60 | loop fusion | bytes 6291456 | tf_op jit(solution)/shard_map/slice | solution.py:107
  161.9 3.0 %copy.82 = bf16[4,256,1,1,8,64]{1,5,4,0,3,2:T(8,128)(2,1)} copy(bf16[4,256,1,1,8,64]{5,4,3,1,0,2:T(8,128)(2,1)} %get-tuple-element.5) | data formatting | bytes 2097152
  164.9 2.2 copy.83
  167.1 1.9 copy.84
  169.1 2.5 fusion.26
  171.6 0.0 copy-start.6
  171.6 2.8 %fusion.42 = (f32[4,8,256]{2,1,0:T(8,128)S(1)}, f32[4,8,256,256]{2,3,1,0:T(8,128)S(1)}) fusion(f32[4,8,256,256]{2,3,1,0:T(8,128)S(1)} %fusion.26, pred[256,256]{0,1:T(8,128)(4,1)S(1)} %iota_compare_fusion), kind=kOutput, calls=%fused_computation.63 | output fusion | flops 14680319 | bytes 16875520 | tf_op jit(solution)/shard_map/sub | solution.py:24
  174.5 0.0 copy-done.6
  174.5 0.9 fusion.25
  175.4 0.8 copy.67
  176.3 0.2 copy.87
  176.5 0.2 copy-done.12
  176.6 1.3 convolution_convert_fusion.2
  178.0 0.2 copy.68
  178.1 31.7 %all_to_all.49 = bf16[4,8,32,1,1,1,1024]{6,2,0,5,4,3,1:T(8,128)(2,1)S(1)} all-to-all(bf16[4,8,32,1,1,1,1024]{6,2,0,5,4,3,1:T(8,128)(2,1)S(1)} %copy.68), channel_id=1, replica_groups=mesh['grp'=8,'dev'=32] {'grp'}, dimensions={1} | all-to-all | bytes 4194304 | tf_op jit(solution)/shard_map/all_to_all | solution.py:64
  209.9 1.2 copy.69
  211.0 53.8 %all_to_all.50 = bf16[4,1,32,8,1,1,1024]{6,3,0,5,4,1,2:T(8,128)(2,1)S(1)} all-to-all(bf16[4,1,32,8,1,1,1024]{6,3,0,5,4,1,2:T(8,128)(2,1)S(1)} %copy.69), channel_id=1, replica_groups=mesh['grp'=8,'dev'=32] {'dev'}, dimensions={2} | all-to-all | bytes 4194304 | tf_op jit(solution)/shard_map/all_to_all | solution.py:63
  264.8 0.5 convert_bitcast_fusion
  265.3 0.0 copy-start.5
  265.3 2.4 copy.70
  267.7 0.0 copy-start.1
  267.7 0.0 copy-done.5
  267.7 2.1 fusion.21
  (12 shorter events, 0.1 us)
Async XLA Ops:
  0.0 5.2 %copy-start = (bf16[1024,1536]{1,0:T(8,128)(2,1)S(1)}, bf16[1024,1536]{1,0:T(8,128)(2,1)}, u32[]{:S(2)}) copy-start(bf16[1024,1536]{1,0:T(8,128)(2,1)} %param.9) | copy-start | bytes 9437188
  0.0 4.5 %copy-start.2 = (bf16[4,1,256,1024]{3,2,1,0:T(8,128)(2,1)S(1)}, bf16[4,1,256,1024]{3,2,1,0:T(8,128)(2,1)}, u32[]{:S(2)}) copy-start(bf16[4,1,256,1024]{3,2,1,0:T(8,128)(2,1)} %param.7) | copy-start | bytes 6291460
  0.0 4.5 %copy-start.8 = (f32[1024]{0:T(1024)S(1)}, f32[1024]{0:T(1024)}, u32[]{:S(2)}) copy-start(f32[1024]{0:T(1024)} %param.8) | copy-start | bytes 12292
  34.0 6.3 %copy-start.7 = (bf16[4,256,1,8,64]{1,4,3,0,2:T(8,128)(2,1)S(1)}, bf16[4,256,1,8,64]{1,4,3,0,2:T(8,128)(2,1)}, u32[]{:S(2)}) copy-start(bf16[4,256,1,8,64]{1,4,3,0,2:T(8,128)(2,1)} %copy.79) | copy-start | bytes 3145732
  40.4 1.6 copy-start.3
  40.4 1.8 copy-start.11
  43.5 33.9 %copy-start.4 = (bf16[4,256,1024]{2,1,0:T(8,128)(2,1)}, bf16[4,256,1024]{2,1,0:T(8,128)(2,1)S(1)}, u32[]{:S(2)}) copy-start(bf16[4,256,1024]{2,1,0:T(8,128)(2,1)S(1)} %fusion.14) | copy-start | bytes 6291460
  80.4 59.4 %all-to-all-start.1 = ((bf16[4,8,1,32,1024]{4,1,0,2,3:T(8,128)(2,1)}), bf16[4,8,1,32,1024]{4,1,0,2,3:T(8,128)(2,1)S(1)}, u32[]{:S(2)}, u32[]{:S(2)}) async-start(bf16[4,8,1,32,1024]{4,1,0,2,3:T(8,128)(2,1)} %copy.60), calls=%async_computation.1 | async-start | bytes 4194304 | tf_op jit(solution)/shard_map/all_to_all | solution.py:83
  141.8 3.4 %copy-start.9 = (f32[1024]{0:T(1024)S(1)}, f32[1024]{0:T(1024)}, u32[]{:S(2)}) copy-start(f32[1024]{0:T(1024)} %param.11) | copy-start | bytes 12292
  145.1 1.9 copy-start.10
  171.6 2.9 %copy-start.6 = (bf16[4,256,1,1,8,64]{1,5,4,0,3,2:T(8,128)(2,1)S(1)}, bf16[4,256,1,1,8,64]{1,5,4,0,3,2:T(8,128)(2,1)}, u32[]{:S(2)}) copy-start(bf16[4,256,1,1,8,64]{1,5,4,0,3,2:T(8,128)(2,1)} %copy.82) | copy-start | bytes 3145732
  175.4 1.2 copy-start.12
  265.3 2.5 copy-start.5
  267.7 2.2 copy-start.1
where the time goes:
time: 273 us; the launch traced here: 270 us
  blocking collectives  118 us (43%)
  local copies, waits for them, and re-layouts  51.8 us (19%)
  waiting for transfers between devices  48.1 us (18%)
  other arithmetic  22.7 us (8%)
  matrix products  18 us (7%)
  starting transfers between devices  11.2 us (4%)
    all_to_all x1, blocking collectives, to_frames(): lax.all_to_all(lax.all_to_all(sectioned, 'grp', split_axis=1, concat_axis...  53.8 us
    all_to_all x1, waiting for transfers between devices, per_device(): lax.all_to_all(lax.all_to_all(sectioned, 'grp', split_axis=3, concat_axis...  48.1 us
    all_to_all x1, blocking collectives, per_device(): lax.all_to_all(sectioned, 'grp', split_axis=3, concat_axis=1, tiled=True)  32.2 us
    all_to_all x1, blocking collectives, to_frames(): lax.all_to_all(sectioned, 'grp', split_axis=1, concat_axis=3, tiled=True)  31.7 us
    unnamed x35, local copies, waits for them, and re-layouts  17 us
    all_to_all x1, starting transfers between devices, per_device(): lax.all_to_all(lax.all_to_all(sectioned, 'grp', split_axis=3, concat_axis...  11.2 us
    sub x2, other arithmetic, soft_weights(): exponent = jnp.where(allowed, jnp.exp(scores - top_score), 0.0)  9.16 us
    reshape x1, local copies, waits for them, and re-layouts, spatial_layer(): projected.astype(jnp.bfloat16)  8.86 us
  transfers between devices with their start and end apart: 1, of which 1 were waited for; matrix products, arithmetic and copies ran while one was open for 0% of the time, Pallas kernels for 0%

commit v1 on v0

v1 whole, which is shorter than its diff:
```python
import functools

import jax
import jax.numpy as jnp
from jax import lax
from jax.experimental import pallas as pl
from jax.experimental.pallas import tpu as pltpu
from jax.sharding import PartitionSpec as P

HEADS = 8
HEAD_DIM = 64
ATTN = HEADS * HEAD_DIM
CORES = 2
X_SIZE = 4
UNIT = 4

norm_epsilon = 1e-06
masked_score = -1e30
exp2_scale = HEAD_DIM ** (-0.5) * 1.4426950408889634
MESH = pl.DeviceIdType.MESH


def norm_rows(rows, gain):
    centre = jnp.mean(rows, axis=-1, keepdims=True)
    shifted = rows - centre
    spread = jnp.mean(shifted * shifted, axis=-1, keepdims=True)
    return shifted * lax.rsqrt(spread + norm_epsilon) * gain


def soft_context(scores, values):
    top = jnp.max(scores, axis=-1, keepdims=True)
    exponent = jnp.exp2((scores - top) * exp2_scale)
    total = jnp.sum(exponent, axis=-1, keepdims=True)
    context = jnp.dot(exponent.astype(jnp.bfloat16), values, preferred_element_type=jnp.float32)
    return context * (1.0 / total)


def scores_of(queries, keys):
    return lax.dot_general(
        queries, keys, (((1,), (1,)), ((), ())), preferred_element_type=jnp.float32
    )


def layer_kernel(
    dims,
    video_hbm, space_gain, space_project_hbm, space_output_hbm,
    time_gain, time_project_hbm, time_output_hbm,
    out_hbm,
    video, space_project, space_output, time_project, time_output,
    normed, space_q, space_kv, space_ctx, mixed, outgoing, incoming,
    wide, time_q, time_k, time_v, bias, ctx_wide, ctx_out, ctx_in, result,
    video_sem, weight_sem, send_sem, recv_sem, back_send_sem, back_recv_sem, out_sem,
):
    xs, ys, zs, cs = dims
    groups = ys * zs * cs
    devices = xs * groups
    clips = xs
    patches = groups * UNIT
    width = video.shape[-1]
    pairs = HEADS // 2
    grp = lax.axis_index("grp")
    dev = lax.axis_index("dev")
    y = grp // cs
    core = grp % cs
    z = dev // xs
    x = dev % xs
    kind = (x + y + z) % clips
    my_group = (z * ys + y) * cs + core

    barrier = pltpu.get_barrier_semaphore()

    def greet(k, carry):
        other_grp = (grp + k // (xs * zs)) % (ys * cs)
        other_dev = (dev + k % (xs * zs)) % (xs * zs)
        pl.semaphore_signal(
            barrier, inc=1, device_id=(other_grp, other_dev), device_id_type=MESH
        )
        return carry

    lax.fori_loop(1, devices, greet, 0)

    def video_copy(step):
        clip = (step + kind) % clips
        return pltpu.make_async_copy(
            video_hbm.at[clip, 0], video.at[step], video_sem.at[step]
        )

    weights = [
        pltpu.make_async_copy(space_project_hbm, space_project, weight_sem.at[0]),
        pltpu.make_async_copy(space_output_hbm, space_output, weight_sem.at[1]),
        pltpu.make_async_copy(time_project_hbm, time_project, weight_sem.at[2]),
        pltpu.make_async_copy(time_output_hbm, time_output, weight_sem.at[3]),
    ]
    video_copy(0).start()
    weights[0].start()
    weights[1].start()
    for step in range(1, clips):
        video_copy(step).start()
    weights[2].start()
    weights[3].start()

    block = min(32, patches)
    row_blocks = patches // block

    def displaced(step, j):
        turn = j % zs
        rest = j // zs
        half = (turn + 1) // 2
        dz = (zs // 2 + zs + jnp.where(turn % 2 == 1, -half, half)) % zs
        dy = rest % ys
        dc = rest // ys
        dx = (step + 2 * clips + zs * clips - dy - dz) % clips
        return dx, dy, dz, dc

    def send_step(step):
        def send(j, carry):
            dx, dy, dz, dc = displaced(step, j)
            there_x = (x + dx) % xs
            there_y = (y + dy) % ys
            there_z = (z + dz) % zs
            there_c = (core + dc) % cs
            group = (there_z * ys + there_y) * cs + there_c
            is_self = (dx == 0) & (dy == 0) & (dz == 0) & (dc == 0)

            @pl.when(is_self)
            def _():
                pltpu.make_async_copy(
                    outgoing.at[step, group], incoming.at[step, j], recv_sem.at[step]
                ).start()

            @pl.when(jnp.logical_not(is_self))
            def _():
                pltpu.make_async_remote_copy(
                    src_ref=outgoing.at[step, group],
                    dst_ref=incoming.at[step, j],
                    send_sem=send_sem.at[step],
                    recv_sem=recv_sem.at[step],
                    device_id=(there_y * cs + there_c, there_z * xs + there_x),
                    device_id_type=MESH,
                ).start()

            return carry

        lax.fori_loop(0, groups, send, 0)

    def send_back(step):
        def send(j, carry):
            dx, dy, dz, dc = displaced(step, j)
            there_x = (x + xs - dx) % xs
            there_y = (y + ys - dy) % ys
            there_z = (z + zs - dz) % zs
            there_c = (core + cs - dc) % cs
            is_self = (dx == 0) & (dy == 0) & (dz == 0) & (dc == 0)

            @pl.when(is_self)
            def _():
                pltpu.make_async_copy(
                    ctx_out.at[step, j], ctx_in.at[step, my_group], back_recv_sem.at[step]
                ).start()

            @pl.when(jnp.logical_not(is_self))
            def _():
                pltpu.make_async_remote_copy(
                    src_ref=ctx_out.at[step, j],
                    dst_ref=ctx_in.at[step, my_group],
                    send_sem=back_send_sem.at[step],
                    recv_sem=back_recv_sem.at[step],
                    device_id=(there_y * cs + there_c, there_z * xs + there_x),
                    device_id_type=MESH,
                ).start()

            return carry

        lax.fori_loop(0, groups, send, 0)

    low_half = lax.broadcasted_iota(jnp.int32, (1, 128), 1) < HEAD_DIM
    low_halves = lax.broadcasted_iota(jnp.int32, (1, ATTN), 1) % 128 < HEAD_DIM

    def spatial(step):
        video_copy(step).wait()

        def norm_block(b, carry):
            rows = pl.ds(pl.multiple_of(b * block, block), block)
            normed[rows, :] = norm_rows(
                video[step, rows, :].astype(jnp.float32), space_gain[...]
            ).astype(jnp.bfloat16)
            return carry

        lax.fori_loop(0, row_blocks, norm_block, 0)

        @pl.when(step == 0)
        def _():
            weights[0].wait()

        queries = jnp.dot(
            normed[...], space_project[:, :ATTN], preferred_element_type=jnp.float32
        )
        space_q[0] = jnp.where(low_halves, queries, 0.0).astype(jnp.bfloat16)
        space_q[1] = jnp.where(low_halves, 0.0, queries).astype(jnp.bfloat16)

        def project(t, carry):
            columns = pl.ds(pl.multiple_of(t * 256, 256), 256)
            there = pl.ds(pl.multiple_of(ATTN + t * 256, 256), 256)
            space_kv[:, columns] = jnp.dot(
                normed[...], space_project[:, there], preferred_element_type=jnp.float32
            ).astype(jnp.bfloat16)
            return carry

        lax.fori_loop(0, 2 * ATTN // 256, project, 0)

        def attend(pair, carry):
            lanes = pl.ds(pl.multiple_of(pair * 128, 128), 128)
            value_lanes = pl.ds(pl.multiple_of(ATTN + pair * 128, 128), 128)
            keys = space_kv[:, lanes]
            values = space_kv[:, value_lanes]
            low = soft_context(scores_of(space_q[0, :, lanes], keys), values)
            high = soft_context(scores_of(space_q[1, :, lanes], keys), values)
            space_ctx[:, lanes] = jnp.where(low_half, low, high).astype(jnp.bfloat16)
            return carry

        lax.fori_loop(0, pairs, attend, 0)

        @pl.when(step == 0)
        def _():
            weights[1].wait()

        def finish(b, carry):
            rows = pl.ds(pl.multiple_of(b * block, block), block)
            update = jnp.dot(
                space_ctx[rows, :], space_output[...], preferred_element_type=jnp.float32
            )
            sums = (video[step, rows, :].astype(jnp.float32) + update).astype(jnp.bfloat16)
            mixed[step, rows, :] = sums
            after = norm_rows(sums.astype(jnp.float32), time_gain[...])
            there = pl.ds(pl.multiple_of(b * (block // UNIT), block // UNIT), block // UNIT)
            outgoing[step, there] = after.reshape(block // UNIT, UNIT, width).astype(
                jnp.bfloat16
            )
            return carry

        lax.fori_loop(0, row_blocks, finish, 0)

    def first_half(step, carry):
        spatial(step)

        @pl.when(step == 0)
        def _():
            pl.semaphore_wait(barrier, devices - 1)

        send_step(step)
        return carry

    lax.fori_loop(0, clips, first_half, 0)

    def frames(axis):
        slot = lax.broadcasted_iota(jnp.int32, (devices, devices), axis)
        step = slot // groups
        dx, dy, dz, dc = displaced(step, slot % groups)
        from_x = (x + xs - dx) % xs
        from_y = (y + ys - dy) % ys
        from_z = (z + zs - dz) % zs
        from_c = (core + cs - dc) % cs
        return ((from_y * cs + from_c) * zs + from_z) * xs + from_x

    bias[...] = jnp.where(frames(1) <= frames(0), 0.0, masked_score)

    weights[2].wait()
    weights[3].wait()

    def arrive(step, carry):
        pltpu.make_async_copy(incoming.at[step], incoming.at[step], recv_sem.at[step]).wait()
        flat = incoming[step].reshape(patches, width)
        normed[...] = flat

        def project(t, carry):
            columns = pl.ds(pl.multiple_of(t * 256, 256), 256)
            heads = jnp.dot(
                normed[...], time_project[:, columns], preferred_element_type=jnp.float32
            )
            wide[2 * t] = heads[:, :128]
            wide[2 * t + 1] = heads[:, 128:]
            return carry

        lax.fori_loop(0, 3 * ATTN // 256, project, 0)
        slots = pl.ds(pl.multiple_of(step * groups, groups), groups)
        for p in range(UNIT):
            mine = pl.ds(p, groups, stride=UNIT)
            for pair in range(pairs):
                lanes = pl.ds(pair * 128, 128)
                queries = wide[pair, mine, :]
                time_q[0, p, slots, lanes] = jnp.where(low_half, queries, 0.0).astype(jnp.bfloat16)
                time_q[1, p, slots, lanes] = jnp.where(low_half, 0.0, queries).astype(jnp.bfloat16)
                time_k[p, slots, lanes] = wide[pairs + pair, mine, :].astype(jnp.bfloat16)
                time_v[p, slots, lanes] = wide[2 * pairs + pair, mine, :].astype(jnp.bfloat16)
        return carry

    lax.fori_loop(0, clips, arrive, 0)

    def temporal(step, carry):
        slots = pl.ds(pl.multiple_of(step * groups, groups), groups)
        hidden = bias[slots, :]

        for p in range(UNIT):
            for pair in range(pairs):
                lanes = pl.ds(pair * 128, 128)
                keys = time_k[p, :, lanes]
                values = time_v[p, :, lanes]
                low = soft_context(scores_of(time_q[0, p, slots, lanes], keys) + hidden, values)
                high = soft_context(scores_of(time_q[1, p, slots, lanes], keys) + hidden, values)
                ctx_wide[pair, pl.ds(p, groups, stride=UNIT), :] = jnp.where(low_half, low, high)
        for pair in range(pairs):
            ctx_out[step, :, :, pl.ds(pair * 128, 128)] = (
                ctx_wide[pair].reshape(groups, UNIT, 128).astype(jnp.bfloat16)
            )
        send_back(step)
        return carry

    lax.fori_loop(0, clips, temporal, 0)

    def out_copy(step):
        clip = (step + kind) % clips
        return pltpu.make_async_copy(result.at[step], out_hbm.at[clip, 0], out_sem.at[step])

    def finish(step, carry):
        pltpu.make_async_copy(ctx_in.at[step], ctx_in.at[step], back_recv_sem.at[step]).wait()
        space_ctx[...] = ctx_in[step].reshape(patches, ATTN)

        def block_out(b, carry):
            rows = pl.ds(pl.multiple_of(b * block, block), block)
            update = jnp.dot(
                space_ctx[rows, :], time_output[...], preferred_element_type=jnp.float32
            ).astype(jnp.bfloat16)
            result[step, rows, :] = (
                mixed[step, rows, :].astype(jnp.float32) + update.astype(jnp.float32)
            ).astype(jnp.bfloat16)
            return carry

        lax.fori_loop(0, row_blocks, block_out, 0)
        out_copy(step).start()
        return carry

    lax.fori_loop(0, clips, finish, 0)

    for step in range(clips):
        sent = pl.ds(0, groups - 1 if step == 0 else groups)
        pltpu.make_async_copy(
            outgoing.at[step, sent], outgoing.at[step, sent], send_sem.at[step]
        ).wait()
        pltpu.make_async_copy(
            ctx_out.at[step, sent], ctx_out.at[step, sent], back_send_sem.at[step]
        ).wait()
        out_copy(step).wait()


def solution(mesh):
    group_count = mesh.shape["grp"]
    member_count = mesh.shape["dev"]
    dims = (X_SIZE, group_count // CORES, member_count // X_SIZE, CORES)

    def per_device(
        video_in, space_gain, space_project, space_output, time_gain, time_project, time_output
    ):
        clips, _, patches, width = video_in.shape
        groups = patches // UNIT
        frames = group_count * member_count
        bf16 = jnp.bfloat16
        anywhere = pl.BlockSpec(memory_space=pl.ANY)
        local = pl.BlockSpec(memory_space=pltpu.VMEM)
        dma = pltpu.SemaphoreType.DMA
        return pl.pallas_call(
            functools.partial(layer_kernel, dims),
            out_shape=jax.ShapeDtypeStruct(video_in.shape, bf16),
            in_specs=[anywhere, local, anywhere, anywhere, local, anywhere, anywhere],
            out_specs=anywhere,
            scratch_shapes=[
                pltpu.VMEM((clips, patches, width), bf16),
                pltpu.VMEM((width, 3 * ATTN), bf16),
                pltpu.VMEM((ATTN, width), bf16),
                pltpu.VMEM((width, 3 * ATTN), bf16),
                pltpu.VMEM((ATTN, width), bf16),
                pltpu.VMEM((patches, width), bf16),
                pltpu.VMEM((2, patches, ATTN), bf16),
                pltpu.VMEM((patches, 2 * ATTN), bf16),
                pltpu.VMEM((patches, ATTN), bf16),
                pltpu.VMEM((clips, patches, width), bf16),
                pltpu.VMEM((clips, groups, UNIT, width), bf16),
                pltpu.VMEM((clips, groups, UNIT, width), bf16),
                pltpu.VMEM((3 * ATTN // 128, patches, 128), jnp.float32),
                pltpu.VMEM((2, UNIT, frames, ATTN), bf16),
                pltpu.VMEM((UNIT, frames, ATTN), bf16),
                pltpu.VMEM((UNIT, frames, ATTN), bf16),
                pltpu.VMEM((frames, frames), jnp.float32),
                pltpu.VMEM((ATTN // 128, patches, 128), jnp.float32),
                pltpu.VMEM((clips, groups, UNIT, ATTN), bf16),
                pltpu.VMEM((clips, groups, UNIT, ATTN), bf16),
                pltpu.VMEM((clips, patches, width), bf16),
                dma((clips,)),
                dma((4,)),
                dma((clips,)),
                dma((clips,)),
                dma((clips,)),
                dma((clips,)),
                dma((clips,)),
            ],
            compiler_params=pltpu.CompilerParams(
                collective_id=0, has_side_effects=True, vmem_limit_bytes=60 * 1024 * 1024
            ),
            name="video_layer",
        )(
            video_in,
            space_gain.reshape(1, width),
            space_project,
            space_output,
            time_gain.reshape(1, width),
            time_project,
            time_output,
        )

    placed = P(None, ("grp", "dev"))
    return jax.shard_map(
        per_device,
        mesh=mesh,
        in_specs=(placed, P(), P(), P(), P(), P(), P()),
        out_specs=placed,
        check_vma=False,
    )
```

time: 273 us -> 144 us (0.53); the launches traced: 270 us -> 144 us
  Pallas kernels: 0 us -> 141 us
  blocking collectives: 118 us -> 0 us
  local copies, waits for them, and re-layouts: 51.8 us -> 3.08 us
  waiting for transfers between devices: 48.1 us -> 0 us
  other arithmetic: 22.7 us -> 0 us
  matrix products: 18 us -> 0 us
  starting transfers between devices: 11.2 us -> 0 us
    pallas_call x0 -> x1, Pallas kernels: none -> 141 us  [per_device(): pl.pallas_call(functools.partial(layer_kernel, dims), out_shape=jax.Shape...]
    all_to_all x3 -> x0, blocking collectives: 118 us -> none  [the longest x1 53.8 us: to_frames(): lax.all_to_all(lax.all_to_all(sectioned, 'grp', split_axis=1, concat_axis...]
    all_to_all x1 -> x0, waiting for transfers between devices: 48.1 us -> none  [per_device(): lax.all_to_all(lax.all_to_all(sectioned, 'grp', split_axis=3, concat_axis...]
    dot_general x8 -> x0, matrix products: 18 us -> none  [the longest x1 4.89 us: spatial_layer(): jnp.dot(normed.reshape(-1, model_width), space_project, preferred_element...]
    reshape x3 -> x0, local copies, waits for them, and re-layouts: 16.4 us -> none  [the longest x1 8.86 us: spatial_layer(): projected.astype(jnp.bfloat16)]
    unnamed x35 -> x1, local copies, waits for them, and re-layouts: 17 us -> 3.08 us
    all_to_all x1 -> x0, starting transfers between devices: 11.2 us -> none  [per_device(): lax.all_to_all(lax.all_to_all(sectioned, 'grp', split_axis=3, concat_axis...]
    slice x2 -> x0, local copies, waits for them, and re-layouts: 10.6 us -> none  [the longest x1 5.34 us: per_device(): values_here = projected[:, :, :, 2]]
  transfers between devices with their start and end apart: 1 -> 0, of which waited for: 1 -> 0; matrix products, arithmetic and copies ran while one was open for 0% -> 0% of each run, Pallas kernels for 0% -> 0%
where the time goes in v1:
time: 144 us
  Pallas kernels  141 us (98%)
  local copies, waits for them, and re-layouts  3.08 us (2%)
    pallas_call x1, Pallas kernels, per_device(): pl.pallas_call(functools.partial(layer_kernel, dims), out_shape=jax.Shape...  141 us
    unnamed x1, local copies, waits for them, and re-layouts  3.08 us

profile of v1, /device:TPU:1, one launch (start us, length us, event | category | flops | bytes accessed | tf_op | source)
XLA Modules:
  0.0 143.9 jit_solution(11530536146499590351)
XLA Ops:
  0.0 140.8 %video_layer.1 = bf16[4,1,256,1024]{3,2,1,0:T(8,128)(2,1)} custom-call(bf16[4,1,256,1024]{3,2,1,0:T(8,128)(2,1)} %video_hbm.1, f32[1,1024]{1,0:T(1,128)} %bitcast.2, bf16[1024,1536]{1,0:T(8,128)(2,1)} %space_project_hbm.1, bf16[512,1024]{1,0:T(8,128)(2,1)} %space_output_hbm.1, f32[1,1024]{1,0:T(1,128)} %bitcast.3, bf16[1024,1536]{1,0:T(8,128)(2,1)} %time_project_hbm.1, ...), custom_call_target="tpu_custom_call" | custom-call | tf_op jit(solution)/shard_map/video_layer/pallas_call | solution.py:370
  140.8 3.1 %copy.9 = bf16[4,1,256,1024]{3,2,1,0:T(8,128)(2,1)} copy(bf16[4,1,256,1024]{3,2,1,0:T(8,128)(2,1)} %video_layer.1) | data formatting | bytes 4194304

commit v2 on v1

--- a/solution.py
+++ b/solution.py
@@ -12,7 +12,8 @@
 ATTN = HEADS * HEAD_DIM
 CORES = 2
 X_SIZE = 4
-UNIT = 4
+KINDS = 2
+UNIT = KINDS
 
 norm_epsilon = 1e-06
 masked_score = -1e30
@@ -52,9 +53,11 @@
     video_sem, weight_sem, send_sem, recv_sem, back_send_sem, back_recv_sem, out_sem,
 ):
     xs, ys, zs, cs = dims
-    groups = ys * zs * cs
-    devices = xs * groups
-    clips = xs
+    along = xs // KINDS
+    groups = ys * zs * cs * along
+    devices = KINDS * groups
+    clips = video.shape[0]
+    phases = clips // KINDS
     patches = groups * UNIT
     width = video.shape[-1]
     pairs = HEADS // 2
@@ -64,23 +67,16 @@
     core = grp % cs
     z = dev // xs
     x = dev % xs
-    kind = (x + y + z) % clips
-    my_group = (z * ys + y) * cs + core
+    kind = (x + y + z) % KINDS
+    my_group = ((z * ys + y) * cs + core) * along + x // KINDS
 
     barrier = pltpu.get_barrier_semaphore()
 
-    def greet(k, carry):
-        other_grp = (grp + k // (xs * zs)) % (ys * cs)
-        other_dev = (dev + k % (xs * zs)) % (xs * zs)
-        pl.semaphore_signal(
-            barrier, inc=1, device_id=(other_grp, other_dev), device_id_type=MESH
-        )
-        return carry
-
-    lax.fori_loop(1, devices, greet, 0)
+    def clip_of(step):
+        return step // KINDS * KINDS + (step + kind) % KINDS
 
     def video_copy(step):
-        clip = (step + kind) % clips
+        clip = clip_of(step)
         return pltpu.make_async_copy(
             video_hbm.at[clip, 0], video.at[step], video_sem.at[step]
         )
@@ -99,79 +95,103 @@
     weights[2].start()
     weights[3].start()
 
+    def greet(k, carry):
+        other_y = lax.rem(y + lax.rem(k, ys), ys)
+        other_x = lax.rem(x + lax.div(k, ys), xs)
+        for dz in range(zs):
+            other_dev = lax.rem(z + dz, zs) * xs + other_x
+            for dc in range(cs):
+                other_grp = other_y * cs + lax.rem(core + dc, cs)
+
+                @pl.when((k > 0) | (dz + dc > 0))
+                def _():
+                    pl.semaphore_signal(
+                        barrier, inc=1, device_id=(other_grp, other_dev), device_id_type=MESH
+                    )
+
+        return carry
+
+    lax.fori_loop(0, xs * ys, greet, 0)
+
     block = min(32, patches)
     row_blocks = patches // block
 
-    def displaced(step, j):
-        turn = j % zs
-        rest = j // zs
-        half = (turn + 1) // 2
-        dz = (zs // 2 + zs + jnp.where(turn % 2 == 1, -half, half)) % zs
-        dy = rest % ys
-        dc = rest // ys
-        dx = (step + 2 * clips + zs * clips - dy - dz) % clips
-        return dx, dy, dz, dc
+    turns = [zs // 2]
+    for far in range(zs // 2 - 1, 0, -1):
+        turns += [far, zs - far]
+    turns += [0]
+    rounds = groups // zs
+
+    def displaced(step, rest, dz):
+        dy = lax.rem(rest, ys)
+        dc = lax.rem(lax.div(rest, ys), cs)
+        far = lax.div(rest, ys * cs)
+        dx = far * KINDS + lax.rem(step + ys * zs - dy - dz, KINDS)
+        return dx, dy, dc
+
+    def exchange(step, sign, local_copy, remote_copy):
+        def one_round(rest, carry):
+            for turn, dz in enumerate(turns):
+                dx, dy, dc = displaced(step, rest, dz)
+                there_x = lax.rem(x + xs + sign * dx, xs)
+                there_y = lax.rem(y + ys + sign * dy, ys)
+                there_z = lax.rem(z + zs + sign * dz, zs)
+                there_c = lax.rem(core + cs + sign * dc, cs)
+                group = ((there_z * ys + there_y) * cs + there_c) * along + lax.div(
+                    there_x, KINDS
+                )
+                there = (there_y * cs + there_c, there_z * xs + there_x)
+                j = rest * zs + turn
+                if dz == 0:
+                    is_self = (rest == 0) & (dx == 0)
+
+                    @pl.when(is_self)
+                    def _():
+                        local_copy(j, group).start()
+
+                    @pl.when(jnp.logical_not(is_self))
+                    def _():
+                        remote_copy(j, group, there).start()
+
+                else:
+                    remote_copy(j, group, there).start()
+            return carry
+
+        lax.fori_loop(0, rounds, one_round, 0)
 
     def send_step(step):
-        def send(j, carry):
-            dx, dy, dz, dc = displaced(step, j)
-            there_x = (x + dx) % xs
-            there_y = (y + dy) % ys
-            there_z = (z + dz) % zs
-            there_c = (core + dc) % cs
-            group = (there_z * ys + there_y) * cs + there_c
-            is_self = (dx == 0) & (dy == 0) & (dz == 0) & (dc == 0)
-
-            @pl.when(is_self)
-            def _():
-                pltpu.make_async_copy(
-                    outgoing.at[step, group], incoming.at[step, j], recv_sem.at[step]
-                ).start()
-
-            @pl.when(jnp.logical_not(is_self))
-            def _():
-                pltpu.make_async_remote_copy(
-                    src_ref=outgoing.at[step, group],
-                    dst_ref=incoming.at[step, j],
-                    send_sem=send_sem.at[step],
-                    recv_sem=recv_sem.at[step],
-                    device_id=(there_y * cs + there_c, there_z * xs + there_x),
-                    device_id_type=MESH,
-                ).start()
-
-            return carry
-
-        lax.fori_loop(0, groups, send, 0)
+        exchange(
+            step,
+            1,
+            lambda j, group: pltpu.make_async_copy(
+                outgoing.at[step, group], incoming.at[step, j], recv_sem.at[step]
+            ),
+            lambda j, group, there: pltpu.make_async_remote_copy(
+                src_ref=outgoing.at[step, group],
+                dst_ref=incoming.at[step, j],
+                send_sem=send_sem.at[step],
+                recv_sem=recv_sem.at[step],
+                device_id=there,
+                device_id_type=MESH,
+            ),
+        )
 
     def send_back(step):
-        def send(j, carry):
-            dx, dy, dz, dc = displaced(step, j)
-            there_x = (x + xs - dx) % xs
-            there_y = (y + ys - dy) % ys
-            there_z = (z + zs - dz) % zs
-            there_c = (core + cs - dc) % cs
-            is_self = (dx == 0) & (dy == 0) & (dz == 0) & (dc == 0)
-
-            @pl.when(is_self)
-            def _():
-                pltpu.make_async_copy(
-                    ctx_out.at[step, j], ctx_in.at[step, my_group], back_recv_sem.at[step]
-                ).start()
-
-            @pl.when(jnp.logical_not(is_self))
-            def _():
-                pltpu.make_async_remote_copy(
-                    src_ref=ctx_out.at[step, j],
-                    dst_ref=ctx_in.at[step, my_group],
-                    send_sem=back_send_sem.at[step],
-                    recv_sem=back_recv_sem.at[step],
-                    device_id=(there_y * cs + there_c, there_z * xs + there_x),
-                    device_id_type=MESH,
-                ).start()
-
-            return carry
-
-        lax.fori_loop(0, groups, send, 0)
+        exchange(
+            step,
+            -1,
+            lambda j, group: pltpu.make_async_copy(
+                ctx_out.at[step, j], ctx_in.at[step, my_group], back_recv_sem.at[step]
+            ),
+            lambda j, group, there: pltpu.make_async_remote_copy(
+                src_ref=ctx_out.at[step, j],
+                dst_ref=ctx_in.at[step, my_group],
+                send_sem=back_send_sem.at[step],
+                recv_sem=back_recv_sem.at[step],
+                device_id=there,
+                device_id_type=MESH,
+            ),
+        )
 
     low_half = lax.broadcasted_iota(jnp.int32, (1, 128), 1) < HEAD_DIM
     low_halves = lax.broadcasted_iota(jnp.int32, (1, ATTN), 1) % 128 < HEAD_DIM
@@ -224,14 +244,21 @@
         def _():
             weights[1].wait()
 
+        def mix(t, carry):
+            columns = pl.ds(pl.multiple_of(t * 256, 256), 256)
+            update = jnp.dot(
+                space_ctx[...], space_output[:, columns], preferred_element_type=jnp.float32
+            )
+            mixed[step, :, columns] = (
+                video[step, :, columns].astype(jnp.float32) + update
+            ).astype(jnp.bfloat16)
+            return carry
+
+        lax.fori_loop(0, width // 256, mix, 0)
+
         def finish(b, carry):
             rows = pl.ds(pl.multiple_of(b * block, block), block)
-            update = jnp.dot(
-                space_ctx[rows, :], space_output[...], preferred_element_type=jnp.float32
-            )
-            sums = (video[step, rows, :].astype(jnp.float32) + update).astype(jnp.bfloat16)
-            mixed[step, rows, :] = sums
-            after = norm_rows(sums.astype(jnp.float32), time_gain[...])
+            after = norm_rows(mixed[step, rows, :].astype(jnp.float32), time_gain[...])
             there = pl.ds(pl.multiple_of(b * (block // UNIT), block // UNIT), block // UNIT)
             outgoing[step, there] = after.reshape(block // UNIT, UNIT, width).astype(
                 jnp.bfloat16
@@ -254,8 +281,10 @@
 
     def frames(axis):
         slot = lax.broadcasted_iota(jnp.int32, (devices, devices), axis)
-        step = slot // groups
-        dx, dy, dz, dc = displaced(step, slot % groups)
+        turn = slot % zs
+        half = (turn + 1) // 2
+        dz = (zs // 2 + zs + jnp.where(turn % 2 == 1, -half, half)) % zs
+        dx, dy, dc = displaced(slot // groups, slot % groups // zs, dz)
         from_x = (x + xs - dx) % xs
         from_y = (y + ys - dy) % ys
         from_z = (z + zs - dz) % zs
@@ -267,7 +296,8 @@
     weights[2].wait()
     weights[3].wait()
 
-    def arrive(step, carry):
+    def arrive(phase, k):
+        step = phase * KINDS + k
         pltpu.make_async_copy(incoming.at[step], incoming.at[step], recv_sem.at[step]).wait()
         flat = incoming[step].reshape(patches, width)
         normed[...] = flat
@@ -282,67 +312,81 @@
             return carry
 
         lax.fori_loop(0, 3 * ATTN // 256, project, 0)
-        slots = pl.ds(pl.multiple_of(step * groups, groups), groups)
+        slots = pl.ds(pl.multiple_of(k * groups, groups), groups)
         for p in range(UNIT):
             mine = pl.ds(p, groups, stride=UNIT)
             for pair in range(pairs):
                 lanes = pl.ds(pair * 128, 128)
                 queries = wide[pair, mine, :]
-                time_q[0, p, slots, lanes] = jnp.where(low_half, queries, 0.0).astype(jnp.bfloat16)
-                time_q[1, p, slots, lanes] = jnp.where(low_half, 0.0, queries).astype(jnp.bfloat16)
+                time_q[p, 0, slots, lanes] = jnp.where(low_half, queries, 0.0).astype(jnp.bfloat16)
+                time_q[p, 1, slots, lanes] = jnp.where(low_half, 0.0, queries).astype(jnp.bfloat16)
                 time_k[p, slots, lanes] = wide[pairs + pair, mine, :].astype(jnp.bfloat16)
                 time_v[p, slots, lanes] = wide[2 * pairs + pair, mine, :].astype(jnp.bfloat16)
-        return carry
-
-    lax.fori_loop(0, clips, arrive, 0)
-
-    def temporal(step, carry):
-        slots = pl.ds(pl.multiple_of(step * groups, groups), groups)
-        hidden = bias[slots, :]
+
+    def temporal(phase, k):
+        step = phase * KINDS + k
+        slots = pl.ds(pl.multiple_of(k * groups, groups), groups)
 
         for p in range(UNIT):
             for pair in range(pairs):
                 lanes = pl.ds(pair * 128, 128)
                 keys = time_k[p, :, lanes]
                 values = time_v[p, :, lanes]
-                low = soft_context(scores_of(time_q[0, p, slots, lanes], keys) + hidden, values)
-                high = soft_context(scores_of(time_q[1, p, slots, lanes], keys) + hidden, values)
-                ctx_wide[pair, pl.ds(p, groups, stride=UNIT), :] = jnp.where(low_half, low, high)
+                queries = time_q[p, :, slots, lanes].reshape(2 * groups, 128)
+                scores = scores_of(queries, keys).reshape(2, groups, devices)
+                scores = (scores + bias[slots, :][None]).reshape(2 * groups, devices)
+                both = soft_context(scores, values)
+                ctx_wide[pair, pl.ds(p, groups, stride=UNIT), :] = jnp.where(
+                    low_half, both[:groups], both[groups:]
+                )
         for pair in range(pairs):
             ctx_out[step, :, :, pl.ds(pair * 128, 128)] = (
                 ctx_wide[pair].reshape(groups, UNIT, 128).astype(jnp.bfloat16)
             )
         send_back(step)
+
+    def second_half(phase, carry):
+        def take(k, inner):
+            arrive(phase, k)
+            return inner
+
+        lax.fori_loop(0, KINDS, take, 0)
+
+        def give(k, inner):
+            temporal(phase, k)
+            return inner
+
+        lax.fori_loop(0, KINDS, give, 0)
         return carry
 
-    lax.fori_loop(0, clips, temporal, 0)
+    lax.fori_loop(0, phases, second_half, 0)
 
     def out_copy(step):
-        clip = (step + kind) % clips
+        clip = clip_of(step)
         return pltpu.make_async_copy(result.at[step], out_hbm.at[clip, 0], out_sem.at[step])
 
     def finish(step, carry):
         pltpu.make_async_copy(ctx_in.at[step], ctx_in.at[step], back_recv_sem.at[step]).wait()
         space_ctx[...] = ctx_in[step].reshape(patches, ATTN)
 
-        def block_out(b, carry):
-            rows = pl.ds(pl.multiple_of(b * block, block), block)
+        def block_out(t, carry):
+            columns = pl.ds(pl.multiple_of(t * 256, 256), 256)
             update = jnp.dot(
-                space_ctx[rows, :], time_output[...], preferred_element_type=jnp.float32
+                space_ctx[...], time_output[:, columns], preferred_element_type=jnp.float32
             ).astype(jnp.bfloat16)
-            result[step, rows, :] = (
-                mixed[step, rows, :].astype(jnp.float32) + update.astype(jnp.float32)
+            result[step, :, columns] = (
+                mixed[step, :, columns].astype(jnp.float32) + update.astype(jnp.float32)
             ).astype(jnp.bfloat16)
             return carry
 
-        lax.fori_loop(0, row_blocks, block_out, 0)
+        lax.fori_loop(0, width // 256, block_out, 0)
         out_copy(step).start()
         return carry
 
     lax.fori_loop(0, clips, finish, 0)
 
     for step in range(clips):
-        sent = pl.ds(0, groups - 1 if step == 0 else groups)
+        sent = pl.ds(0, groups - 1 if step % KINDS == 0 else groups)
         pltpu.make_async_copy(
             outgoing.at[step, sent], outgoing.at[step, sent], send_sem.at[step]
         ).wait()
@@ -386,7 +430,7 @@
                 pltpu.VMEM((clips, groups, UNIT, width), bf16),
                 pltpu.VMEM((clips, groups, UNIT, width), bf16),
                 pltpu.VMEM((3 * ATTN // 128, patches, 128), jnp.float32),
-                pltpu.VMEM((2, UNIT, frames, ATTN), bf16),
+                pltpu.VMEM((UNIT, 2, frames, ATTN), bf16),
                 pltpu.VMEM((UNIT, frames, ATTN), bf16),
                 pltpu.VMEM((UNIT, frames, ATTN), bf16),
                 pltpu.VMEM((frames, frames), jnp.float32),

time: 144 us -> 98.9 us (0.69)
  Pallas kernels: 141 us -> 95.7 us
    pallas_call x1, Pallas kernels: 141 us -> 95.7 us  [per_device(): pl.pallas_call(functools.partial(layer_kernel, dims), out_shape=jax.Shape...]
where the time goes in v2:
time: 98.9 us; the launch traced here: 98.8 us
  Pallas kernels  95.7 us (97%)
  local copies, waits for them, and re-layouts  3.08 us (3%)
    pallas_call x1, Pallas kernels, per_device(): pl.pallas_call(functools.partial(layer_kernel, dims), out_shape=jax.Shape...  95.7 us
    unnamed x1, local copies, waits for them, and re-layouts  3.08 us

profile of v2, /device:TPU:1, one launch (start us, length us, event | category | flops | bytes accessed | tf_op | source)
XLA Modules:
  0.0 98.8 jit_solution(10766395301902838766)
XLA Ops:
  0.0 95.7 %video_layer.1 = bf16[4,1,256,1024]{3,2,1,0:T(8,128)(2,1)} custom-call(bf16[4,1,256,1024]{3,2,1,0:T(8,128)(2,1)} %video_hbm.1, f32[1,1024]{1,0:T(1,128)} %bitcast.2, bf16[1024,1536]{1,0:T(8,128)(2,1)} %space_project_hbm.1, bf16[512,1024]{1,0:T(8,128)(2,1)} %space_output_hbm.1, f32[1,1024]{1,0:T(1,128)} %bitcast.3, bf16[1024,1536]{1,0:T(8,128)(2,1)} %time_project_hbm.1, ...), custom_call_target="tpu_custom_call" | custom-call | tf_op jit(solution)/shard_map/video_layer/pallas_call | solution.py:414
  95.7 3.1 %copy.9 = bf16[4,1,256,1024]{3,2,1,0:T(8,128)(2,1)} copy(bf16[4,1,256,1024]{3,2,1,0:T(8,128)(2,1)} %video_layer.1) | data formatting | bytes 4194304

commit v3 on v2

--- a/solution.py
+++ b/solution.py
@@ -31,9 +31,10 @@
 def soft_context(scores, values):
     top = jnp.max(scores, axis=-1, keepdims=True)
     exponent = jnp.exp2((scores - top) * exp2_scale)
-    total = jnp.sum(exponent, axis=-1, keepdims=True)
-    context = jnp.dot(exponent.astype(jnp.bfloat16), values, preferred_element_type=jnp.float32)
-    return context * (1.0 / total)
+    beside = jnp.concatenate([values, jnp.ones_like(values)], axis=1)
+    both = jnp.dot(exponent.astype(jnp.bfloat16), beside, preferred_element_type=jnp.float32)
+    lanes = values.shape[1]
+    return both[:, :lanes] * (1.0 / both[:, lanes:])
 
 
 def scores_of(queries, keys):
@@ -206,7 +207,7 @@
             ).astype(jnp.bfloat16)
             return carry
 
-        lax.fori_loop(0, row_blocks, norm_block, 0)
+        lax.fori_loop(0, row_blocks, norm_block, 0, unroll=4)
 
         @pl.when(step == 0)
         def _():
@@ -226,7 +227,7 @@
             ).astype(jnp.bfloat16)
             return carry
 
-        lax.fori_loop(0, 2 * ATTN // 256, project, 0)
+        lax.fori_loop(0, 2 * ATTN // 256, project, 0, unroll=2)
 
         def attend(pair, carry):
             lanes = pl.ds(pl.multiple_of(pair * 128, 128), 128)
@@ -238,7 +239,7 @@
             space_ctx[:, lanes] = jnp.where(low_half, low, high).astype(jnp.bfloat16)
             return carry
 
-        lax.fori_loop(0, pairs, attend, 0)
+        lax.fori_loop(0, pairs, attend, 0, unroll=4)
 
         @pl.when(step == 0)
         def _():
@@ -254,7 +255,7 @@
             ).astype(jnp.bfloat16)
             return carry
 
-        lax.fori_loop(0, width // 256, mix, 0)
+        lax.fori_loop(0, width // 256, mix, 0, unroll=2)
 
         def finish(b, carry):
             rows = pl.ds(pl.multiple_of(b * block, block), block)
@@ -265,7 +266,7 @@
             )
             return carry
 
-        lax.fori_loop(0, row_blocks, finish, 0)
+        lax.fori_loop(0, row_blocks, finish, 0, unroll=4)
 
     def first_half(step, carry):
         spatial(step)

time: 98.9 us -> 93.1 us (0.941)
  Pallas kernels: 95.7 us -> 89.9 us
    pallas_call x1, Pallas kernels: 95.7 us -> 89.9 us  [per_device(): pl.pallas_call(functools.partial(layer_kernel, dims), out_shape=jax.Shape...]
where the time goes in v3:
time: 93.1 us; the launch traced here: 93 us
  Pallas kernels  89.9 us (97%)
  local copies, waits for them, and re-layouts  3.08 us (3%)
    pallas_call x1, Pallas kernels, per_device(): pl.pallas_call(functools.partial(layer_kernel, dims), out_shape=jax.Shape...  89.9 us
    unnamed x1, local copies, waits for them, and re-layouts  3.08 us

profile of v3, /device:TPU:1, one launch (start us, length us, event | category | flops | bytes accessed | tf_op | source)
XLA Modules:
  0.0 93.0 jit_solution(4785594427317912440)
XLA Ops:
  0.0 89.9 %video_layer.1 = bf16[4,1,256,1024]{3,2,1,0:T(8,128)(2,1)} custom-call(bf16[4,1,256,1024]{3,2,1,0:T(8,128)(2,1)} %video_hbm.1, f32[1,1024]{1,0:T(1,128)} %bitcast.2, bf16[1024,1536]{1,0:T(8,128)(2,1)} %space_project_hbm.1, bf16[512,1024]{1,0:T(8,128)(2,1)} %space_output_hbm.1, f32[1,1024]{1,0:T(1,128)} %bitcast.3, bf16[1024,1536]{1,0:T(8,128)(2,1)} %time_project_hbm.1, ...), custom_call_target="tpu_custom_call" | custom-call | tf_op jit(solution)/shard_map/video_layer/pallas_call | solution.py:415
  89.9 3.1 %copy.9 = bf16[4,1,256,1024]{3,2,1,0:T(8,128)(2,1)} copy(bf16[4,1,256,1024]{3,2,1,0:T(8,128)(2,1)} %video_layer.1) | data formatting | bytes 4194304
